TPU v7x, 512 devices: a whole 4x4x16 slice. The times are simulated.
512 devices in a mesh: nodes: 64 (over x, z), heads: 8 (over y, core).
Axes of the slice: x: 4, y: 4, z: 16, core: 2. Of those that a mesh axis runs over, the one named last changes fastest.
Arguments:
- hidden: bfloat16 [64, 7168], P('nodes'), may hold values from -6 to 6
- norm_gain: float32 [7168], replicated, may hold values from 0.1 to 1.9
- qkv_weight: bfloat16 [7168, 56, 384], P('nodes', 'heads'), may hold values from -0.0625 to 0.0625
- out_weight: bfloat16 [7168, 7168], P('heads', 'nodes'), may hold values from -0.0625 to 0.0625
- prefix_keys: bfloat16 [256, 128, 56, 128], P('nodes', None, 'heads'), may hold values from -1000 to 1000
- prefix_values: bfloat16 [256, 128, 56, 128], P('nodes', None, 'heads'), may hold values from -3 to 3
- leaf_keys: bfloat16 [64, 64, 56, 128], P('nodes', None, 'heads'), may hold values from -1000 to 1000
- leaf_values: bfloat16 [64, 64, 56, 128], P('nodes', None, 'heads'), may hold values from -3 to 3
- piece_node: int32 [256], replicated, may hold values from 0 to 35, as said below
- mid_parent: int32 [32], replicated, may hold values from 0 to 3
- leaf_parent: int32 [64], replicated, may hold values from 0 to 31
- leaf_len: int32 [64], replicated, may hold values from 1 to 64
- sink_len: int32 [64], replicated, may hold values from 0 to 4
- window_len: int32 [64], replicated, may hold values from 2048 to 4096
Outputs:
- layer_out: bfloat16 [64, 7168], P('heads', 'nodes')
Inputs may be any that keep to these rules, and one draw needn't show every extreme that they name: `piece_node`: every root owns some pieces; a middle node may own none.
All inputs are finite; a program needn't handle non-finite values.
Results may differ from a plain program's by a relative error of at most 0.007.
The roundings to bfloat16 on the way count: a program that leaves them out, or rounds other values in their place, can miss the bound.
Values may be sent and summed in bfloat16 or wider, within the bound.
A program may use at most 64 MiB of HBM per device.

v0:
```python
import math
import jax
import jax.numpy as jnp
from jax import lax
from jax.sharding import PartitionSpec as P

SEG = 128
ROOTS = 4
MIDS = 32
epsilon = 1e-05
negative_fill = -1e30


def joined(part, axis, combine):
    gathered = jax.tree.map(lambda a: lax.all_gather(a, axis), part)

    def take(source):
        return jax.tree.map(lambda a: lax.dynamic_index_in_dim(a, source, 0, False), gathered)

    return lax.fori_loop(
        1, lax.axis_size(axis), lambda source, state: combine(state, take(source)), take(0)
    )


def layer_norm(hidden, norm_gain):
    values = hidden.astype(jnp.float32)
    mean_value = jnp.mean(values, axis=1, keepdims=True)
    centered = values - mean_value
    variance = jnp.mean(centered * centered, axis=1, keepdims=True)
    return (centered * lax.rsqrt(variance + epsilon) * norm_gain[None, :]).astype(jnp.bfloat16)


def lookup(lookup_table, chosen):
    positions = jnp.arange(lookup_table.shape[0], dtype=jnp.int32)
    picked = jnp.where(chosen[:, None] == positions[None, :], lookup_table[None, :], 0)
    return jnp.sum(picked, axis=1)


def tree_rows(piece_node, mid_parent, leaf_parent, leaf_len):
    node_ids = jnp.arange(ROOTS + MIDS, dtype=jnp.int32)
    counts = jnp.sum((piece_node[:, None] == node_ids[None, :]).astype(jnp.int32), axis=0)
    root_node = lookup(mid_parent, leaf_parent)
    mid_node = leaf_parent + ROOTS
    root_len = SEG * lookup(counts, root_node)
    mid_len = SEG * lookup(counts, mid_node)
    finish = root_len + mid_len + leaf_len
    return (root_node, mid_node, root_len, finish)


def piece_rank(piece_node, chosen):
    all_pieces = jnp.arange(piece_node.shape[0], dtype=jnp.int32)
    nodes_here = lookup(piece_node, chosen)
    same = (piece_node[None, :] == nodes_here[:, None]) & (all_pieces[None, :] < chosen[:, None])
    return (nodes_here, jnp.sum(same.astype(jnp.int32), axis=1))


def prefix_allowed(
    node_block, rank_block, root_node, mid_node, root_len, finish, sink_len, window_len
):
    offsets = jnp.arange(SEG, dtype=jnp.int32)
    rel_pos = rank_block[:, None] * SEG + offsets[None, :]
    at_root = node_block[None, :] == root_node[:, None]
    at_mid = node_block[None, :] == mid_node[:, None]
    token_pos = rel_pos[None, :, :] + jnp.where(at_mid, root_len[:, None], 0)[:, :, None]
    inside = (token_pos < sink_len[:, None, None]) | (
        token_pos >= (finish - window_len)[:, None, None]
    )
    return ((at_root | at_mid)[:, :, None] & inside)[:, None, :, :]


def leaf_allowed(finish, leaf_len, sink_len, window_len, leaf_max):
    offsets = jnp.arange(leaf_max, dtype=jnp.int32)
    token_pos = (finish - leaf_len)[:, None] + offsets[None, :]
    inside = (token_pos < sink_len[:, None]) | (token_pos >= (finish - window_len)[:, None])
    return (inside & (offsets[None, :] < leaf_len[:, None]))[:, None, :]


def combine(first_part, second_part):
    highest = jnp.maximum(first_part[0], second_part[0])
    factor_one = jnp.exp(first_part[0] - highest)
    factor_two = jnp.exp(second_part[0] - highest)
    totals = first_part[1] * factor_one + second_part[1] * factor_two
    summed = first_part[2] * factor_one[..., None] + second_part[2] * factor_two[..., None]
    return (highest, totals, summed)


def weigh(scores, allowed, axes):
    masked = jnp.where(allowed, scores, negative_fill)
    maxima = jnp.max(masked, axis=axes)
    expanded = maxima
    for axis_pos in axes:
        expanded = jnp.expand_dims(expanded, axis_pos)
    weights = jnp.where(allowed, jnp.exp(masked - expanded), 0.0).astype(jnp.bfloat16)
    return (maxima, weights)


def on_device(
    hidden,
    norm_gain,
    qkv_weight,
    out_weight,
    prefix_keys,
    prefix_values,
    leaf_keys,
    leaf_values,
    piece_node,
    mid_parent,
    leaf_parent,
    leaf_len,
    sink_len,
    window_len,
):
    node_index = lax.axis_index("nodes")
    req_dev = hidden.shape[0]
    heads_dev = qkv_weight.shape[1]
    head_size = qkv_weight.shape[2] // 3
    seg_dev = prefix_keys.shape[0]
    first_row = node_index * req_dev
    score_scale = 1.0 / math.sqrt(head_size)
    normed = layer_norm(hidden, norm_gain)
    columns = lax.all_to_all(normed, "nodes", split_axis=1, concat_axis=0, tiled=True)
    width_here = columns.shape[1]
    flat_weight = qkv_weight.reshape(width_here, heads_dev * 3 * head_size)
    mixed_rows = lax.psum_scatter(
        jnp.dot(columns, flat_weight, preferred_element_type=jnp.float32),
        "nodes",
        scatter_dimension=0,
        tiled=True,
    )
    mixed_rows = mixed_rows.astype(jnp.bfloat16).reshape(req_dev, heads_dev, 3, head_size)
    query_here = mixed_rows[:, :, 0]
    key_new = mixed_rows[:, :, 1]
    value_new = mixed_rows[:, :, 2]
    query_all = lax.all_gather(query_here, "nodes", axis=0, tiled=True)
    root_node, mid_node, root_len, finish = tree_rows(piece_node, mid_parent, leaf_parent, leaf_len)
    chosen = node_index * seg_dev + jnp.arange(seg_dev, dtype=jnp.int32)
    node_block, rank_block = piece_rank(piece_node, chosen)
    scores = (
        jnp.einsum("rhd,pshd->rhps", query_all, prefix_keys, preferred_element_type=jnp.float32)
        * score_scale
    )
    allowed = prefix_allowed(
        node_block, rank_block, root_node, mid_node, root_len, finish, sink_len, window_len
    )
    maxima, weights = weigh(scores, allowed, (2, 3))
    totals = jnp.sum(weights.astype(jnp.float32), axis=(2, 3))
    summed = jnp.einsum(
        "rhps,pshd->rhd", weights, prefix_values, preferred_element_type=jnp.float32
    )
    merged = joined((maxima, totals, summed), "nodes", combine)
    merged = tuple((lax.dynamic_slice_in_dim(member, first_row, req_dev, 0) for member in merged))
    finish_here = lax.dynamic_slice_in_dim(finish, first_row, req_dev, 0)
    leaf_here = lax.dynamic_slice_in_dim(leaf_len, first_row, req_dev, 0)
    sink_here = lax.dynamic_slice_in_dim(sink_len, first_row, req_dev, 0)
    window_here = lax.dynamic_slice_in_dim(window_len, first_row, req_dev, 0)
    leaf_scores = (
        jnp.einsum("rhd,rjhd->rhj", query_here, leaf_keys, preferred_element_type=jnp.float32)
        * score_scale
    )
    leaf_mask = leaf_allowed(finish_here, leaf_here, sink_here, window_here, leaf_keys.shape[1])
    leaf_max, leaf_weights = weigh(leaf_scores, leaf_mask, (2,))
    leaf_part = (
        leaf_max,
        jnp.sum(leaf_weights.astype(jnp.float32), axis=2),
        jnp.einsum("rhj,rjhd->rhd", leaf_weights, leaf_values, preferred_element_type=jnp.float32),
    )
    own_score = (
        jnp.sum(query_here.astype(jnp.float32) * key_new.astype(jnp.float32), axis=2) * score_scale
    )
    own_part = (
        own_score,
        jnp.ones((req_dev, heads_dev), jnp.float32),
        value_new.astype(jnp.float32),
    )
    merged = combine(combine(merged, leaf_part), own_part)
    attended = (
        (merged[2] / merged[1][..., None])
        .astype(jnp.bfloat16)
        .reshape(req_dev, heads_dev * head_size)
    )
    out_rows = jnp.dot(
        lax.all_gather(attended, "nodes", axis=0, tiled=True),
        out_weight,
        preferred_element_type=jnp.float32,
    )
    return lax.psum_scatter(out_rows, "heads", scatter_dimension=0, tiled=True).astype(jnp.bfloat16)


def solution(mesh):
    return jax.shard_map(
        on_device,
        mesh=mesh,
        in_specs=(
            P("nodes", None),
            P(),
            P("nodes", "heads", None),
            P("heads", "nodes"),
            P("nodes", None, "heads", None),
            P("nodes", None, "heads", None),
            P("nodes", None, "heads", None),
            P("nodes", None, "heads", None),
            P(),
            P(),
            P(),
            P(),
            P(),
            P(),
        ),
        out_specs=P("heads", "nodes"),
        check_vma=False,
    )
```

profile of v0, /device:TPU:2, one launch (start us, length us, event | category | flops | bytes accessed | tf_op | source)
XLA Modules:
  0.0 810.2 jit_solution(8103925422148323476)
XLA Ops:
  6.5 1.5 convert_reduce_fusion.3
  8.7 1.4 multiply_reduce_fusion
  12.4 18.6 %all-to-all-start = ((bf16[1,64,112]{2,0,1:T(2,128)(2,1)}), bf16[1,64,112]{2,0,1:T(2,128)(2,1)S(1)}, u32[]{:S(2)}, u32[]{:S(2)}) async-start(bf16[1,64,112]{2,0,1:T(2,128)(2,1)} %all_to_all.15), calls=%async_computation | async-start | bytes 65536 | tf_op jit(solution)/shard_map/all_to_all | solution.py:121
  36.9 1.1 copy.86
  38.0 1.3 dynamic-slice
  39.3 5.2 all-to-all-done
  44.7 257.9 %all-reduce.3 = bf16[64,2688]{1,0:T(8,128)(2,1)S(1)} all-reduce(f32[64,2688]{1,0:T(8,128)S(1)} %fusion.19), channel_id=6, replica_groups=mesh['nodes'=64,'heads'=8] {'nodes'}, use_global_device_ids=true, to_apply=%region_8.9.clone | all-reduce | flops 172032 | bytes 1032192
  303.3 120.7 %all-gather = bf16[64,7,1,128]{3,1,2,0:T(8,128)(2,1)S(1)} all-gather(bf16[1,7,1,128]{3,1,2,0:T(8,128)(2,1)S(1)} %copy.68), channel_id=2, replica_groups=mesh['nodes'=64,'heads'=8] {'nodes'}, dimensions={0}, use_global_device_ids=true | all-gather | bytes 116480 | tf_op jit(solution)/shard_map/all_gather | solution.py:134
  424.5 2.2 convolution_bitcast_fusion
  426.8 1.2 dynamic_slice.68
  428.0 1.3 dynamic_slice.70
  429.3 1.3 dynamic_slice.69
  433.7 1.3 dynamic-slice.2
  435.7 1.3 compare_and_fusion
  437.0 78.9 %all-gather.4 = f32[64,64,7]{1,2,0:T(8,128)S(1)} all-gather(f32[1,64,7]{1,2,0:T(8,128)S(1)} %bitcast.134), channel_id=3, replica_groups=mesh['nodes'=64,'heads'=8] {'nodes'}, dimensions={0}, use_global_device_ids=true | all-gather | bytes 116480 | tf_op jit(solution)/shard_map/all_gather | solution.py:15
  516.2 82.0 %all-gather.5 = f32[64,64,7]{1,2,0:T(8,128)S(1)} all-gather(f32[1,64,7]{1,2,0:T(8,128)S(1)} %bitcast.136), channel_id=4, replica_groups=mesh['nodes'=64,'heads'=8] {'nodes'}, dimensions={0}, use_global_device_ids=true | all-gather | bytes 116480 | tf_op jit(solution)/shard_map/all_gather | solution.py:15
  598.2 1.1 fusion.16
  599.8 1.0 fusion.14
  602.3 95.5 %while.19 = (s32[]{:T(128)}, f32[64,7]{0,1:T(8,128)S(1)}, f32[64,7]{0,1:T(8,128)S(1)}, f32[64,7,128]{2,1,0:T(8,128)S(1)}, f32[64,64,7]{1,2,0:T(8,128)S(1)}, /*in...) while((s32[]{:T(128)}, f32[64,7]{0,1:T(8,128)S(1)}, ...), condition=%wide.region_12.13_spmd, body=%wide.region_11.12_spmd.sunk | while | flops 174725 | bytes 1172119 | solution.py:20
  603.8 1.0 constant_dynamic-slice_fusion.4
  606.9 1.0 constant_dynamic-slice_fusion.4
  609.9 1.0 constant_dynamic-slice_fusion.4
  612.9 1.0 constant_dynamic-slice_fusion.4
  615.9 1.0 constant_dynamic-slice_fusion.4
  619.0 1.0 constant_dynamic-slice_fusion.4
  623.5 1.0 constant_dynamic-slice_fusion.4
  626.6 1.0 constant_dynamic-slice_fusion.4
  629.6 1.0 constant_dynamic-slice_fusion.4
  632.6 1.0 constant_dynamic-slice_fusion.4
  635.7 1.0 constant_dynamic-slice_fusion.4
  698.2 80.7 %all-gather.6 = bf16[64,1,896]{2,1,0:T(2,128)(2,1)S(1)} all-gather(bf16[1,1,896]{2,1,0:T(2,128)(2,1)S(1)} %convert_bitcast_fusion), channel_id=1, replica_groups=mesh['nodes'=64,'heads'=8] {'nodes'}, dimensions={0}, use_global_device_ids=true | all-gather | bytes 116480 | tf_op jit(solution)/shard_map/all_gather | solution.py:182
  779.1 23.6 %all-reduce.1 = bf16[64,112]{1,0:T(8,128)(2,1)S(1)} all-reduce(f32[64,112]{1,0:T(8,128)S(1)} %fusion.10), channel_id=7, replica_groups=mesh['nodes'=64,'heads'=8] {'heads'}, use_global_device_ids=true, to_apply=%region_16.17.clone | all-reduce | flops 7168 | bytes 43008
  (350 shorter events, 95.5 us)
Async XLA Ops:
  6.5 417.5 %copy-start = (bf16[4,128,7,128]{3,1,2,0:T(8,128)(2,1)S(1)}, bf16[4,128,7,128]{3,1,2,0:T(8,128)(2,1)}, u32[]{:S(2)}) copy-start(bf16[4,128,7,128]{3,1,2,0:T(8,128)(2,1)} %param.20) | copy-start | bytes 2752516
  6.5 772.4 %copy-start.1 = (bf16[896,112]{0,1:T(8,128)(2,1)S(1)}, bf16[896,112]{0,1:T(8,128)(2,1)}, u32[]{:S(2)}) copy-start(bf16[896,112]{0,1:T(8,128)(2,1)} %param.19) | copy-start | bytes 602116
  12.4 32.1 %all-to-all-start = ((bf16[1,64,112]{2,0,1:T(2,128)(2,1)}), bf16[1,64,112]{2,0,1:T(2,128)(2,1)S(1)}, u32[]{:S(2)}, u32[]{:S(2)}) async-start(bf16[1,64,112]{2,0,1:T(2,128)(2,1)} %all_to_all.15), calls=%async_computation | async-start | bytes 65536 | tf_op jit(solution)/shard_map/all_to_all | solution.py:121
  31.0 570.1 %all-gather.9.cloned.1.call-start = ((), (), s32[]{:S(2)}) async-start(), calls=%async_computation.1 | async-start | bytes 14909440 | tf_op jit(solution)/shard_map/all_gather | solution.py:15
Sparse Core Ops, SparseCore 0:
  426.9 174.2 all-gather.8
where the time goes:
time: 813 us; the launch traced here: 810 us
  blocking collectives  644 us (79%)
  local copies, waits for them, and re-layouts  84.4 us (10%)
  other arithmetic  32.2 us (4%)
  starting transfers between devices  18.7 us (2%)
  between operations  18 us (2%)
    unnamed x2, blocking collectives  281 us
    all_gather x2, blocking collectives, joined(): gathered = jax.tree.map(lambda a: lax.all_gather(a, axis), part)  161 us
    all_gather x1, blocking collectives, on_device(): query_all = lax.all_gather(query_here, 'nodes', axis=0, tiled=True)  121 us
    all_gather x1, blocking collectives, on_device(): lax.all_gather(attended, 'nodes', axis=0, tiled=True)  80.7 us
    dynamic_slice x66, local copies, waits for them, and re-layouts, take(): lax.dynamic_index_in_dim(a, source, 0, False)  61.8 us
    add x63, other arithmetic, combine(): first_part[2] * factor_one[..., None]  19.3 us
    all_to_all x1, starting transfers between devices, on_device(): lax.all_to_all(normed, 'nodes', split_axis=1, concat_axis=0, tiled=True)  18.6 us
  transfers between devices with their start and end apart: 2, of which 2 were waited for; matrix products, arithmetic and copies ran while one was open for 2% of the time, Pallas kernels for 0%

commit v1 on v0

--- a/solution.py
+++ b/solution.py
@@ -131,7 +131,9 @@
     query_here = mixed_rows[:, :, 0]
     key_new = mixed_rows[:, :, 1]
     value_new = mixed_rows[:, :, 2]
-    query_all = lax.all_gather(query_here, "nodes", axis=0, tiled=True)
+    query_all = jnp.concatenate(
+        lax.all_to_all(jnp.stack([query_here] * lax.axis_size("nodes")), "nodes", 0, 0), axis=0
+    )
     root_node, mid_node, root_len, finish = tree_rows(piece_node, mid_parent, leaf_parent, leaf_len)
     chosen = node_index * seg_dev + jnp.arange(seg_dev, dtype=jnp.int32)
     node_block, rank_block = piece_rank(piece_node, chosen)

time: 813 us -> 737 us (0.907)
  blocking collectives: 644 us -> 523 us
  starting transfers between devices: 18.7 us -> 47.7 us
  waiting for transfers between devices: 5.58 us -> 19.7 us
    all_gather x1 -> x0, blocking collectives: 121 us -> none  [on_device(): query_all = lax.all_gather(query_here, 'nodes', axis=0, tiled=True)]
    all_to_all x0 -> x1, starting transfers between devices: none -> 29 us  [on_device(): lax.all_to_all(jnp.stack([query_here] * lax.axis_size('nodes')), 'nodes',...]
    all_to_all x0 -> x1, waiting for transfers between devices: none -> 13.5 us  [on_device(): lax.all_to_all(jnp.stack([query_here] * lax.axis_size('nodes')), 'nodes',...]
  transfers between devices with their start and end apart: 2 -> 3, of which waited for: 2 -> 2; matrix products, arithmetic and copies ran while one was open for 2% -> 2% of each run, Pallas kernels for 0% -> 0%
where the time goes in v1:
time: 737 us; the launch traced here: 734 us
  blocking collectives  523 us (71%)
  local copies, waits for them, and re-layouts  85.1 us (12%)
  starting transfers between devices  47.7 us (6%)
  other arithmetic  32.4 us (4%)
  waiting for transfers between devices  19.7 us (3%)
  between operations  18 us (2%)
    unnamed x2, blocking collectives  282 us
    all_gather x2, blocking collectives, joined(): gathered = jax.tree.map(lambda a: lax.all_gather(a, axis), part)  161 us
    all_gather x1, blocking collectives, on_device(): lax.all_gather(attended, 'nodes', axis=0, tiled=True)  80.6 us
    dynamic_slice x66, local copies, waits for them, and re-layouts, take(): lax.dynamic_index_in_dim(a, source, 0, False)  61.8 us
    all_to_all x1, starting transfers between devices, on_device(): lax.all_to_all(jnp.stack([query_here] * lax.axis_size('nodes')), 'nodes',...  29 us
    add x63, other arithmetic, combine(): first_part[2] * factor_one[..., None]  19.5 us
    all_to_all x1, starting transfers between devices, on_device(): lax.all_to_all(normed, 'nodes', split_axis=1, concat_axis=0, tiled=True)  18.6 us
  transfers between devices with their start and end apart: 3, of which 2 were waited for; matrix products, arithmetic and copies ran while one was open for 2% of the time, Pallas kernels for 0%

profile of v1, /device:TPU:2, one launch (start us, length us, event | category | flops | bytes accessed | tf_op | source)
XLA Modules:
  0.0 733.9 jit_solution(4371355274535095348)
XLA Ops:
  6.5 1.5 convert_reduce_fusion.3
  8.7 1.4 multiply_reduce_fusion
  12.4 18.6 %all-to-all-start = ((bf16[1,64,112]{2,0,1:T(2,128)(2,1)}), bf16[1,64,112]{2,0,1:T(2,128)(2,1)S(1)}, u32[]{:S(2)}, u32[]{:S(2)}) async-start(bf16[1,64,112]{2,0,1:T(2,128)(2,1)} %all_to_all.19), calls=%async_computation | async-start | bytes 65536 | tf_op jit(solution)/shard_map/all_to_all | solution.py:121
  35.8 1.1 copy.80
  37.0 1.3 dynamic-slice
  38.3 6.2 all-to-all-done
  44.7 258.1 %all-reduce.3 = bf16[64,2688]{1,0:T(8,128)(2,1)S(1)} all-reduce(f32[64,2688]{1,0:T(8,128)S(1)} %fusion.19), channel_id=5, replica_groups=mesh['nodes'=64,'heads'=8] {'nodes'}, use_global_device_ids=true, to_apply=%region_8.9.clone | all-reduce | flops 172032 | bytes 1032192
  304.2 29.0 %all-to-all-start.1 = ((bf16[64,1,7,128]{3,2,1,0:T(8,128)(2,1)}), bf16[64,1,7,128]{3,2,1,0:T(8,128)(2,1)S(1)}, u32[]{:S(2)}, u32[]{:S(2)}) async-start(bf16[64,1,7,128]{3,2,1,0:T(8,128)(2,1)} %stack.3), calls=%async_computation.1 | async-start | bytes 262144 | tf_op jit(solution)/shard_map/all_to_all | solution.py:135
  334.3 13.5 %all-to-all-done.1 = bf16[64,1,7,128]{3,2,1,0:T(8,128)(2,1)S(1)} async-done(((bf16[64,1,7,128]{3,2,1,0:T(8,128)(2,1)}), bf16[64,1,7,128]{3,2,1,0:T(8,128)(2,1)S(1)}, u32[]{:S(2)}, u32[]{:S(2)}) %all-to-all-start.1) | async-done | bytes 114720 | tf_op jit(solution)/shard_map/all_to_all | solution.py:135
  348.2 2.2 convolution_bitcast_fusion
  350.5 1.2 dynamic_slice.68
  351.7 1.3 dynamic_slice.70
  353.1 1.3 dynamic_slice.69
  357.4 1.3 dynamic-slice.2
  359.4 1.3 compare_and_fusion
  360.7 1.1 fusion.16
  362.2 1.0 fusion.14
  363.3 79.9 %all-gather.3 = f32[64,64,7]{1,2,0:T(8,128)S(1)} all-gather(f32[1,64,7]{1,2,0:T(8,128)S(1)} %bitcast.137), channel_id=2, replica_groups=mesh['nodes'=64,'heads'=8] {'nodes'}, dimensions={0}, use_global_device_ids=true | all-gather | bytes 116480 | tf_op jit(solution)/shard_map/all_gather | solution.py:15
  443.5 81.1 %all-gather.4 = f32[64,64,7]{1,2,0:T(8,128)S(1)} all-gather(f32[1,64,7]{1,2,0:T(8,128)S(1)} %bitcast.139), channel_id=3, replica_groups=mesh['nodes'=64,'heads'=8] {'nodes'}, dimensions={0}, use_global_device_ids=true | all-gather | bytes 116480 | tf_op jit(solution)/shard_map/all_gather | solution.py:15
  525.8 95.7 %while.19 = (s32[]{:T(128)}, f32[64,7]{0,1:T(8,128)S(1)}, f32[64,7]{0,1:T(8,128)S(1)}, f32[64,7,128]{2,1,0:T(8,128)S(1)}, f32[64,64,7]{1,2,0:T(8,128)S(1)}, /*in...) while((s32[]{:T(128)}, f32[64,7]{0,1:T(8,128)S(1)}, ...), condition=%wide.region_12.13_spmd, body=%wide.region_11.12_spmd.sunk | while | flops 174725 | bytes 1172119 | solution.py:20
  527.4 1.0 constant_dynamic-slice_fusion.4
  530.4 1.0 constant_dynamic-slice_fusion.4
  531.9 1.0 constant_dynamic-slice_fusion.4
  535.0 1.0 constant_dynamic-slice_fusion.4
  539.5 1.0 constant_dynamic-slice_fusion.4
  542.6 1.0 constant_dynamic-slice_fusion.4
  544.1 1.0 constant_dynamic-slice_fusion.4
  547.1 1.0 constant_dynamic-slice_fusion.4
  551.7 1.0 constant_dynamic-slice_fusion.4
  556.2 1.0 constant_dynamic-slice_fusion.4
  622.0 80.6 %all-gather.5 = bf16[64,1,896]{2,1,0:T(2,128)(2,1)S(1)} all-gather(bf16[1,1,896]{2,1,0:T(2,128)(2,1)S(1)} %convert_bitcast_fusion), channel_id=1, replica_groups=mesh['nodes'=64,'heads'=8] {'nodes'}, dimensions={0}, use_global_device_ids=true | all-gather | bytes 116480 | tf_op jit(solution)/shard_map/all_gather | solution.py:184
  702.8 23.6 %all-reduce.1 = bf16[64,112]{1,0:T(8,128)(2,1)S(1)} all-reduce(f32[64,112]{1,0:T(8,128)S(1)} %fusion.10), channel_id=6, replica_groups=mesh['nodes'=64,'heads'=8] {'heads'}, use_global_device_ids=true, to_apply=%region_16.17.clone | all-reduce | flops 7168 | bytes 43008
  (352 shorter events, 97.0 us)
Async XLA Ops:
  6.5 341.2 %copy-start = (bf16[4,128,7,128]{3,1,2,0:T(8,128)(2,1)S(1)}, bf16[4,128,7,128]{3,1,2,0:T(8,128)(2,1)}, u32[]{:S(2)}) copy-start(bf16[4,128,7,128]{3,1,2,0:T(8,128)(2,1)} %param.20) | copy-start | bytes 2752516
  6.5 696.1 %copy-start.1 = (bf16[896,112]{0,1:T(8,128)(2,1)S(1)}, bf16[896,112]{0,1:T(8,128)(2,1)}, u32[]{:S(2)}) copy-start(bf16[896,112]{0,1:T(8,128)(2,1)} %param.19) | copy-start | bytes 602116
  12.4 32.1 %all-to-all-start = ((bf16[1,64,112]{2,0,1:T(2,128)(2,1)}), bf16[1,64,112]{2,0,1:T(2,128)(2,1)S(1)}, u32[]{:S(2)}, u32[]{:S(2)}) async-start(bf16[1,64,112]{2,0,1:T(2,128)(2,1)} %all_to_all.19), calls=%async_computation | async-start | bytes 65536 | tf_op jit(solution)/shard_map/all_to_all | solution.py:121
  304.2 43.5 %all-to-all-start.1 = ((bf16[64,1,7,128]{3,2,1,0:T(8,128)(2,1)}), bf16[64,1,7,128]{3,2,1,0:T(8,128)(2,1)S(1)}, u32[]{:S(2)}, u32[]{:S(2)}) async-start(bf16[64,1,7,128]{3,2,1,0:T(8,128)(2,1)} %stack.3), calls=%async_computation.1 | async-start | bytes 262144 | tf_op jit(solution)/shard_map/all_to_all | solution.py:135
  333.2 191.4 %all-gather.8.cloned.1.call-start = ((), (), s32[]{:S(2)}) async-start(), calls=%async_computation.2 | async-start | bytes 14909440 | tf_op jit(solution)/shard_map/all_gather | solution.py:15
Sparse Core Ops, SparseCore 0:
  350.6 173.8 all-gather.7
